TPU v7x, 32 devices: a whole 2x2x4 slice. The times are simulated.
32 devices in a mesh: gx: 2 (over x), gy: 4 (over z), gz: 4 (over y, core).
Axes of the slice: x: 2, y: 2, z: 4, core: 2. Of those that a mesh axis runs over, the one named last changes fastest.
Arguments:
- positions: float32 [3, 4, 8, 16, 128], P(None, 'gx', 'gy', 'gz'), may hold values from 0 to 11
- velocities: float32 [3, 4, 8, 16, 128], P(None, 'gx', 'gy', 'gz'), may hold values from -0.6 to 0.6
- counts: int32 [4, 8, 16], P('gx', 'gy', 'gz'), may hold values from 96 to 128
Outputs:
- new_velocity: float32 [3, 4, 8, 16, 128], P(None, 'gx', 'gy', 'gz')
- moved: float32 [3, 4, 8, 16, 128], P(None, 'gx', 'gy', 'gz')
All inputs are finite; a program needn't handle non-finite values.
Results may differ from a plain program's by a relative error of at most 0.0003.
Values sent between devices are 32-bit elements; how exact they have to be, the bound alone decides.
No kernel may reach another device: no remote copies, remote signals or barrier semaphores. Data moves between devices by JAX's collectives and lax.ppermute only.
A program may use at most 64 MiB of HBM per device.

v0:
```python
import math
import jax
import jax.numpy as jnp
import numpy as np
from jax import lax
from jax.experimental import pallas as pl
from jax.experimental.pallas import tpu as pltpu
from jax.sharding import PartitionSpec as P

CELL_EDGE = 11.0
HALF_EDGE = 5.5
CUT_SQ = 25.0
WIDTH_DENSITY = 4.0
WIDTH_PAIR = 2.0
SCALE_DENSITY = 0.4
SCALE_PAIR = 0.3
DENSITY_REF = 1.0
TIME_STEP = 0.5
FAR = 4096.0
AXES = ("gx", "gy", "gz")

TOP_E = CUT_SQ / WIDTH_DENSITY
TOP = TOP_E / math.log(2.0)
SPREAD = math.sqrt(TOP / CUT_SQ)
DENSITY_SCALE = SCALE_DENSITY * math.exp(-TOP_E) / TOP**2
PAIR_SHIFT = 4.0 * TOP / CUT_SQ
DENSITY_SHIFT = 8.0 * TOP / CUT_SQ
FORCE_SCALE = -SCALE_PAIR * math.exp(-2.0 * TOP_E) / TOP**2
GRAD_SCALE = SCALE_DENSITY / (2.0 * SCALE_PAIR) * math.exp(TOP_E)

ROWS = 144
TERMS = 32
LEFT_PARTS = (0, 0, 1, 0, 2, 1)
RIGHT_PARTS = (0, 1, 0, 2, 0, 1)
ONE_ROW = 18
NORM_ROW = 21


def neighbour_layers(field, axis, name):
    count = lax.axis_size(name)
    size = field.shape[axis]
    first = lax.slice_in_dim(field, 0, 1, axis=axis)
    last = lax.slice_in_dim(field, size - 1, size, axis=axis)
    if count == 1:
        return last, first
    if count == 2:
        swapped = lax.ppermute(jnp.concatenate([last, first], axis=axis), name, [(0, 1), (1, 0)])
        return lax.slice_in_dim(swapped, 0, 1, axis=axis), lax.slice_in_dim(swapped, 1, 2, axis=axis)
    below = lax.ppermute(last, name, [(d, (d + 1) % count) for d in range(count)])
    above = lax.ppermute(first, name, [(d, (d - 1) % count) for d in range(count)])
    return below, above


def with_halo(field):
    for axis, name in ((1, "gx"), (2, "gy"), (3, "gz")):
        below, above = neighbour_layers(field, axis, name)
        field = jnp.concatenate([below, field, above], axis=axis)
    return field


def split_three(value):
    high = value.astype(jnp.bfloat16).astype(jnp.float32)
    rest = value - high
    middle = rest.astype(jnp.bfloat16).astype(jnp.float32)
    return high, middle, rest - middle


def rows_of(contract_a, contract_b, a, b):
    return lax.dot_general(
        a, b, (((contract_a,), (contract_b,)), ((), ())), preferred_element_type=jnp.float32
    )


def left_matrix():
    pick = np.zeros((TERMS, TERMS), np.float32)
    for comp in range(3):
        where_part = {0: 6 * comp, 1: 6 * comp + 1, 2: 6 * comp + 3}
        for term, part in enumerate(LEFT_PARTS):
            pick[where_part[part], 6 * comp + term] = 0.5
    for term in range(3):
        pick[NORM_ROW + term, ONE_ROW + term] = 1.0
        pick[ONE_ROW, NORM_ROW + term] = 1.0
    return pick


def block_step(extent, slots):
    inner_x, inner_y, inner_z = extent
    ext_y, ext_z = inner_y + 2, inner_z + 2
    cells = (inner_x + 2) * ext_y * ext_z
    vert_x, vert_y, vert_z = inner_x + 1, inner_y + 1, inner_z + 1
    verts = vert_x * vert_y * vert_z
    rows8 = verts * 8
    spare = (cells * slots) // ROWS
    lanes = 8 * slots

    def cell_of(cx, cy, cz):
        return (cx * ext_y + cy) * ext_z + cz

    def vert_of(vx, vy, vz):
        return (vx * vert_y + vy) * vert_z + vz

    def kernel(ext_ref, pos_ref, vel_ref, live_ref, pick_ref, vel_out, moved_out,
               corner, dest, terms, right, left, left_t, grad_row, dens_lane, grad_lane, spare_vert, spare_count):
        for vx in range(vert_x):
            for vy in range(vert_y):
                for vz in range(vert_z):
                    v = vert_of(vx, vy, vz)
                    for kxy in range(4):
                        c = cell_of(vx + kxy // 2, vy + kxy % 2, vz)
                        for comp in range(3):
                            corner[comp, v * 8 + 2 * kxy : v * 8 + 2 * kxy + 2, :] = ext_ref[comp, c : c + 2, :]
        row_id = lax.broadcasted_iota(jnp.int32, (rows8, slots), 0)
        near = None
        for comp in range(3):
            upper = ((row_id >> (2 - comp)) & 1) == 1
            x = corner[comp]
            low = x < HALF_EDGE
            test = jnp.where(upper, jnp.where(low, 1.0, 0.0), jnp.where(low | (x > 0.5 * FAR), 0.0, 1.0))
            near = test if near is None else near * test
        near_b = near.astype(jnp.bfloat16)
        lane_a = lax.broadcasted_iota(jnp.int32, (slots, slots), 0)
        lane_b = lax.broadcasted_iota(jnp.int32, (slots, slots), 1)
        before = jnp.where(lane_a < lane_b, 1.0, 0.0).astype(jnp.bfloat16)
        prefix = jnp.dot(near_b, before, preferred_element_type=jnp.float32)
        total = jnp.dot(near_b, jnp.ones((slots, slots), jnp.bfloat16), preferred_element_type=jnp.float32)
        wide_a = lax.broadcasted_iota(jnp.int32, (rows8, rows8), 0)
        wide_b = lax.broadcasted_iota(jnp.int32, (rows8, rows8), 1)
        earlier = jnp.where((wide_a >> 3 == wide_b >> 3) & (wide_b < wide_a), 1.0, 0.0).astype(jnp.bfloat16)
        offset = jnp.dot(earlier, total.astype(jnp.bfloat16), preferred_element_type=jnp.float32)
        dest[...] = jnp.where(near > 0.5, prefix + offset, -1.0)
        most = jnp.max(offset + total)

        norm = 0.5 * TOP
        one = jnp.ones((rows8, slots), jnp.float32)
        values = []
        for comp in range(3):
            upper = ((row_id >> (2 - comp)) & 1) == 1
            x = (corner[comp] - jnp.where(upper, 0.0, CELL_EDGE)) * SPREAD
            norm = norm - x * x
            parts = split_three(2.0 * x)
            values += [parts[part] for part in RIGHT_PARTS]
        values += [one] * 3 + list(split_three(norm))
        values += [jnp.zeros((rows8, slots), jnp.float32)] * (TERMS - len(values))
        for term in range(TERMS):
            terms[pl.ds(term, rows8, stride=TERMS), :] = values[term]

        def pack(v, carry):
            for k in range(8):
                start = pl.multiple_of((v * 8 + k) * TERMS, TERMS)
                right[v, :, k * slots : (k + 1) * slots] = terms[pl.ds(start, TERMS), :].astype(jnp.bfloat16)
            return carry

        lax.fori_loop(0, verts, pack, 0)
        dens_lane[...] = jnp.zeros(dens_lane.shape, jnp.float32)

        def list_and_density(v, first_row, slot):
            start = pl.multiple_of(v * 8, 8)
            place = dest[pl.ds(start, 8), :] - first_row
            row = lax.broadcasted_iota(jnp.int32, (ROWS, slots), 0).astype(jnp.float32)
            chosen = jnp.concatenate(
                [jnp.where(row == place[k : k + 1, :], 1.0, 0.0).astype(jnp.bfloat16) for k in range(8)], axis=1
            )
            near_right = right[v]
            listed = rows_of(1, 1, chosen, near_right).astype(jnp.bfloat16)
            left_t[slot] = rows_of(1, 1, near_right, chosen).astype(jnp.bfloat16)
            lefts = jnp.dot(listed, pick_ref[...], preferred_element_type=jnp.float32).astype(jnp.bfloat16)
            left[slot] = lefts
            vz = v % vert_z
            vy = (v // vert_z) % vert_y
            vx = v // (vert_z * vert_y)
            sums = None
            for k in range(8):
                s = jnp.dot(lefts, right[v, :, k * slots : (k + 1) * slots], preferred_element_type=jnp.float32)
                s = jnp.maximum(s, 0.0)
                part = jnp.exp2(s) * (s * s)
                sums = part if sums is None else sums + part
                c = cell_of(vx + (k >> 2), vy + ((k >> 1) & 1), vz + (k & 1))
                dens_lane[c] += jnp.sum(part.reshape(ROWS // 8, 8, slots), axis=0)
            density = jnp.sum(sums, axis=1, keepdims=True) * DENSITY_SCALE
            grad = (2.0 * GRAD_SCALE) * (density - (SCALE_DENSITY + DENSITY_REF))
            grad_row[slot] = jnp.broadcast_to(grad, (ROWS, slots))

        def visit(v, carry):
            list_and_density(v, 0.0, v)
            return carry

        lax.fori_loop(0, verts, visit, 0)
        spare_count[0] = 0

        @pl.when(most > ROWS)
        def _():
            def visit_spare(v, carry):
                def chunk(t, inner):
                    listed = dest[pl.ds(pl.multiple_of(v * 8, 8), 8), :]

                    @pl.when(jnp.max(listed) >= (t * ROWS).astype(jnp.float32))
                    def _():
                        slot = spare_count[0]
                        spare_vert[slot] = v
                        spare_count[0] = slot + 1
                        list_and_density(v, (t * ROWS).astype(jnp.float32), verts + slot)

                    return inner

                return lax.fori_loop(1, (lanes + ROWS - 1) // ROWS, chunk, carry)

            lax.fori_loop(0, verts, visit_spare, 0)

        def finish_density(c, carry):
            density = jnp.sum(dens_lane[c], axis=0, keepdims=True) * DENSITY_SCALE
            grad = (2.0 * GRAD_SCALE) * (density - (SCALE_DENSITY + DENSITY_REF))
            grad_lane[c] = jnp.broadcast_to(grad, (8, slots))
            return carry

        lax.fori_loop(0, cells, finish_density, 0)

        def force_sums(v, k, slot, c):
            s = jnp.dot(left[slot], right[v, :, k * slots : (k + 1) * slots], preferred_element_type=jnp.float32)
            s = jnp.maximum(s, 0.0)
            fall = jnp.exp2(s)
            grads = grad_row[slot] + grad_lane[c, 0:1, :]
            push = (fall * s) * (fall * (s + PAIR_SHIFT) + grads * (s + DENSITY_SHIFT))
            high = push.astype(jnp.bfloat16)
            low = (push - high.astype(jnp.float32)).astype(jnp.bfloat16)
            lt = left_t[slot]
            return rows_of(1, 0, lt, high) + rows_of(1, 0, lt, low)

        def shares(sums, k):
            weight = sums[ONE_ROW : ONE_ROW + 1, :]
            out = []
            for comp in range(3):
                base = 6 * comp
                moment = sums[base : base + 1, :] + sums[base + 1 : base + 2, :] + sums[base + 3 : base + 4, :]
                moment = moment * (0.5 / SPREAD)
                if not (k >> (2 - comp)) & 1:
                    moment = moment + CELL_EDGE * weight
                out.append(moment)
            return out + [weight]

        totals = dens_lane

        def visit_cell(n, carry):
            iz = n % inner_z
            iy = (n // inner_z) % inner_y
            ix = n // (inner_z * inner_y)
            c = cell_of(ix + 1, iy + 1, iz + 1)
            gathered = None
            for k in range(8):
                v = vert_of(ix + 1 - (k >> 2), iy + 1 - ((k >> 1) & 1), iz + 1 - (k & 1))
                part = shares(force_sums(v, k, v, c), k)
                gathered = part if gathered is None else [a + b for a, b in zip(gathered, part)]
            totals[c] = jnp.concatenate(gathered + [jnp.zeros((4, slots), jnp.float32)], axis=0)
            return carry

        lax.fori_loop(0, inner_x * inner_y * inner_z, visit_cell, 0)

        def spare_force(e, carry):
            v = spare_vert[e]
            vz = v % vert_z
            vy = (v // vert_z) % vert_y
            vx = v // (vert_z * vert_y)
            for k in range(8):
                cx, cy, cz = vx + (k >> 2), vy + ((k >> 1) & 1), vz + (k & 1)
                own = (
                    (cx >= 1) & (cx <= inner_x) & (cy >= 1) & (cy <= inner_y) & (cz >= 1) & (cz <= inner_z)
                )

                @pl.when(own)
                def _():
                    c = cell_of(cx, cy, cz)
                    part = shares(force_sums(v, k, verts + e, c), k)
                    totals[c] += jnp.concatenate(part + [jnp.zeros((4, slots), jnp.float32)], axis=0)

            return carry

        lax.fori_loop(0, spare_count[0], spare_force, 0)

        for ix in range(inner_x):
            for iy in range(inner_y):
                c = cell_of(ix + 1, iy + 1, 1)
                n = (ix * inner_y + iy) * inner_z
                for iz in range(inner_z):
                    alive = live_ref[n + iz : n + iz + 1, :]
                    both = totals[c + iz]
                    for comp in range(3):
                        x = pos_ref[comp, n + iz : n + iz + 1, :]
                        force = FORCE_SCALE * (both[comp : comp + 1, :] - x * both[3:4, :])
                        velocity = vel_ref[comp, n + iz : n + iz + 1, :] + TIME_STEP * force
                        velocity = jnp.where(alive > 0.5, velocity, 0.0)
                        vel_out[comp, n + iz : n + iz + 1, :] = velocity
                        moved_out[comp, n + iz : n + iz + 1, :] = TIME_STEP * velocity

    own_cells = inner_x * inner_y * inner_z
    vmem = pl.BlockSpec(memory_space=pltpu.VMEM)
    pairs = verts * 8 * ROWS * slots
    return pl.pallas_call(
        kernel,
        out_shape=(jax.ShapeDtypeStruct((3, own_cells, slots), jnp.float32),) * 2,
        in_specs=[vmem] * 5,
        out_specs=(vmem, vmem),
        scratch_shapes=[
            pltpu.VMEM((3, rows8, slots), jnp.float32),
            pltpu.VMEM((rows8, slots), jnp.float32),
            pltpu.VMEM((rows8 * TERMS, slots), jnp.float32),
            pltpu.VMEM((verts, TERMS, lanes), jnp.bfloat16),
            pltpu.VMEM((verts + spare, ROWS, TERMS), jnp.bfloat16),
            pltpu.VMEM((verts + spare, TERMS, ROWS), jnp.bfloat16),
            pltpu.VMEM((verts + spare, ROWS, slots), jnp.float32),
            pltpu.VMEM((cells, 8, slots), jnp.float32),
            pltpu.VMEM((cells, 8, slots), jnp.float32),
            pltpu.SMEM((spare,), jnp.int32),
            pltpu.SMEM((1,), jnp.int32),
        ],
        compiler_params=pltpu.CompilerParams(vmem_limit_bytes=60 * 2**20),
        cost_estimate=pl.CostEstimate(flops=40 * pairs, bytes_accessed=4 * 3 * cells * slots, transcendentals=2 * pairs),
        name="block_step",
    )


def body(positions, velocities, counts):
    comps, size_x, size_y, size_z, slots = positions.shape
    own_cells = size_x * size_y * size_z
    slot_index = lax.broadcasted_iota(jnp.int32, counts.shape + (slots,), 3)
    live = slot_index < counts[..., None]
    shown = jnp.where(live[None], positions, FAR)
    ext = with_halo(shown)
    step = block_step((size_x, size_y, size_z), slots)
    velocity, moved = step(
        ext.reshape(comps, -1, slots),
        positions.reshape(comps, own_cells, slots),
        velocities.reshape(comps, own_cells, slots),
        live.astype(jnp.float32).reshape(own_cells, slots),
        jnp.asarray(left_matrix(), jnp.bfloat16),
    )
    return velocity.reshape(positions.shape), moved.reshape(positions.shape)


def solution(mesh):
    spec = P(None, *AXES, None)
    return jax.shard_map(
        body,
        mesh=mesh,
        in_specs=(spec, spec, P(*AXES)),
        out_specs=(spec, spec),
        check_vma=False,
    )
```

profile of v0, /device:TPU:1, one launch (start us, length us, event | category | flops | bytes accessed | tf_op | source)
XLA Modules:
  0.0 69.1 jit_solution(3922799717235020570)
XLA Ops:
  0.6 0.8 %iota_compare_fusion.1 = pred[2,2,4,128]{3,2,1,0:T(4,128)(4,1)S(1)} fusion(s32[2,2,4]{2,1,0:T(2,128)} %param.6), kind=kLoop, calls=%fused_computation.10 | loop fusion | flops 2048 | bytes 2112 | tf_op jit(solution)/shard_map/lt | solution.py:324
  1.4 0.7 %broadcast_select_fusion = f32[3,2,2,4,128]{4,3,2,1,0:T(4,128)S(1)} fusion(f32[3,2,2,4,128]{4,3,2,1,0:T(4,128)} %param.4, pred[2,2,4,128]{3,2,1,0:T(4,128)(4,1)S(1)} %iota_compare_fusion.1), kind=kLoop, calls=%fused_computation.8 | loop fusion | flops 6144 | bytes 51200 | tf_op jit(solution)/shard_map/jit(_where)/select_n | solution.py:325
  2.2 2.1 %collective-permute-start = (f32[3,2,2,4,128]{4,3,2,1,0:T(4,128)S(1)}, f32[3,2,2,4,128]{4,3,2,1,0:T(4,128)S(1)}, u32[]{:S(2)}, u32[]{:S(2)}) collective-permute-start(f32[3,2,2,4,128]{4,3,2,1,0:T(4,128)S(1)} %pad_maximum_fusion.7), channel_id=1, source_target_pairs={{0,16},{16,0},{1,17},{17,1},{2,18},{18,2},{3,19},{19,3},{4,20},{20... | collective-permute-start | bytes 73736 | tf_op jit(solution)/shard_map/ppermute | solution.py:47
  4.3 1.2 %collective-permute-done = f32[3,2,2,4,128]{4,3,2,1,0:T(4,128)S(1)} collective-permute-done((f32[3,2,2,4,128]{4,3,2,1,0:T(4,128)S(1)}, f32[3,2,2,4,128]{4,3,2,1,0:T(4,128)S(1)}, u32[]{:S(2)}, u32[]{:S(2)}) %collective-permute-start) | collective-permute-done | bytes 24608 | tf_op jit(solution)/shard_map/ppermute | solution.py:47
  5.5 0.0 copy-start
  5.5 1.6 %collective-permute-start.1 = (f32[3,4,1,4,128]{4,3,2,1,0:T(4,128)S(1)}, f32[3,4,1,4,128]{4,3,2,1,0:T(4,128)S(1)}, u32[]{:S(2)}, u32[]{:S(2)}) collective-permute-start(f32[3,4,1,4,128]{4,3,2,1,0:T(4,128)S(1)} %get-tuple-element.8), channel_id=1, source_target_pairs={{0,4},{4,8},{8,12},{12,0},{1,5},{5,9},{9,13},{13,1},{2,6},{6,10},{... | collective-permute-start | bytes 73736 | tf_op jit(solution)/shard_map/ppermute | solution.py:49
  7.1 2.1 %collective-permute-start.2 = (f32[3,4,1,4,128]{4,3,2,1,0:T(4,128)S(1)}, f32[3,4,1,4,128]{4,3,2,1,0:T(4,128)S(1)}, u32[]{:S(2)}, u32[]{:S(2)}) collective-permute-start(f32[3,4,1,4,128]{4,3,2,1,0:T(4,128)S(1)} %get-tuple-element.9), channel_id=1, source_target_pairs={{0,12},{4,0},{8,4},{12,8},{1,13},{5,1},{9,5},{13,9},{2,14},{6,2},{... | collective-permute-start | bytes 73736 | tf_op jit(solution)/shard_map/ppermute | solution.py:50
  9.2 0.0 copy-done
  9.2 0.1 lt.21
  9.3 1.1 %collective-permute-done.1 = f32[3,4,1,4,128]{4,3,2,1,0:T(4,128)S(1)} collective-permute-done((f32[3,4,1,4,128]{4,3,2,1,0:T(4,128)S(1)}, f32[3,4,1,4,128]{4,3,2,1,0:T(4,128)S(1)}, u32[]{:S(2)}, u32[]{:S(2)}) %collective-permute-start.1) | collective-permute-done | bytes 24608 | tf_op jit(solution)/shard_map/ppermute | solution.py:49
  10.4 0.0 collective-permute-done.2
  10.4 4.1 %collective-permute-start.3 = (f32[3,4,4,1,128]{4,3,2,1,0:T(1,128)S(1)}, f32[3,4,4,1,128]{4,3,2,1,0:T(1,128)S(1)}, u32[]{:S(2)}, u32[]{:S(2)}) collective-permute-start(f32[3,4,4,1,128]{4,3,2,1,0:T(1,128)S(1)} %get-tuple-element.6), channel_id=1, source_target_pairs={{0,1},{1,2},{2,3},{3,0},{4,5},{5,6},{6,7},{7,4},{8,9},{9,10},{10,1... | collective-permute-start | bytes 73736 | tf_op jit(solution)/shard_map/ppermute | solution.py:49
  14.5 0.0 collective-permute-start.4
  14.5 0.7 fusion.live_ref
  15.2 0.3 collective-permute-done.3
  15.5 2.3 %collective-permute-done.4 = f32[3,4,4,1,128]{4,3,2,1,0:T(1,128)S(1)} collective-permute-done((f32[3,4,4,1,128]{4,3,2,1,0:T(1,128)S(1)}, f32[3,4,4,1,128]{4,3,2,1,0:T(1,128)S(1)}, u32[]{:S(2)}, u32[]{:S(2)}) %collective-permute-start.4) | collective-permute-done | bytes 24608 | tf_op jit(solution)/shard_map/ppermute | solution.py:50
  17.8 0.1 pad_maximum_fusion
  17.9 0.7 reshape.27.ext_ref
  18.5 50.6 %block_step.1 = (f32[3,16,128]{2,1,0:T(8,128)}, f32[3,16,128]{2,1,0:T(8,128)}) custom-call(f32[3,96,128]{2,1,0:T(8,128)} %reshape.27.ext_ref, f32[3,16,128]{2,1,0:T(8,128)} %bitcast.4, f32[3,16,128]{2,1,0:T(8,128)} %bitcast.5, f32[16,128]{1,0:T(8,128)} %fusion.live_ref, bf16[32,32]{1,0:T(8,128)(2,1)} %constant.4.clone.pick_ref), custom_call_target="tpu_custom_call" | custom-call | flops 265420800 | bytes 147456 | tf_op jit(solution)/shard_map/block_step/pallas_call | solution.py:328
  (6 shorter events, 0.1 us)
Async XLA Ops:
  2.2 3.3 %collective-permute-start = (f32[3,2,2,4,128]{4,3,2,1,0:T(4,128)S(1)}, f32[3,2,2,4,128]{4,3,2,1,0:T(4,128)S(1)}, u32[]{:S(2)}, u32[]{:S(2)}) collective-permute-start(f32[3,2,2,4,128]{4,3,2,1,0:T(4,128)S(1)} %pad_maximum_fusion.7), channel_id=1, source_target_pairs={{0,16},{16,0},{1,17},{17,1},{2,18},{18,2},{3,19},{19,3},{4,20},{20... | collective-permute-start | bytes 73736 | tf_op jit(solution)/shard_map/ppermute | solution.py:47
  5.5 3.7 %copy-start = (s32[2,2,4]{2,1,0:T(2,128)S(1)}, s32[2,2,4]{2,1,0:T(2,128)}, u32[]{:S(2)}) copy-start(s32[2,2,4]{2,1,0:T(2,128)} %param.6) | copy-start | bytes 196
  5.5 4.8 %collective-permute-start.1 = (f32[3,4,1,4,128]{4,3,2,1,0:T(4,128)S(1)}, f32[3,4,1,4,128]{4,3,2,1,0:T(4,128)S(1)}, u32[]{:S(2)}, u32[]{:S(2)}) collective-permute-start(f32[3,4,1,4,128]{4,3,2,1,0:T(4,128)S(1)} %get-tuple-element.8), channel_id=1, source_target_pairs={{0,4},{4,8},{8,12},{12,0},{1,5},{5,9},{9,13},{13,1},{2,6},{6,10},{... | collective-permute-start | bytes 73736 | tf_op jit(solution)/shard_map/ppermute | solution.py:49
  7.1 3.2 %collective-permute-start.2 = (f32[3,4,1,4,128]{4,3,2,1,0:T(4,128)S(1)}, f32[3,4,1,4,128]{4,3,2,1,0:T(4,128)S(1)}, u32[]{:S(2)}, u32[]{:S(2)}) collective-permute-start(f32[3,4,1,4,128]{4,3,2,1,0:T(4,128)S(1)} %get-tuple-element.9), channel_id=1, source_target_pairs={{0,12},{4,0},{8,4},{12,8},{1,13},{5,1},{9,5},{13,9},{2,14},{6,2},{... | collective-permute-start | bytes 73736 | tf_op jit(solution)/shard_map/ppermute | solution.py:50
  10.4 5.1 %collective-permute-start.3 = (f32[3,4,4,1,128]{4,3,2,1,0:T(1,128)S(1)}, f32[3,4,4,1,128]{4,3,2,1,0:T(1,128)S(1)}, u32[]{:S(2)}, u32[]{:S(2)}) collective-permute-start(f32[3,4,4,1,128]{4,3,2,1,0:T(1,128)S(1)} %get-tuple-element.6), channel_id=1, source_target_pairs={{0,1},{1,2},{2,3},{3,0},{4,5},{5,6},{6,7},{7,4},{8,9},{9,10},{10,1... | collective-permute-start | bytes 73736 | tf_op jit(solution)/shard_map/ppermute | solution.py:49
  14.5 3.3 %collective-permute-start.4 = (f32[3,4,4,1,128]{4,3,2,1,0:T(1,128)S(1)}, f32[3,4,4,1,128]{4,3,2,1,0:T(1,128)S(1)}, u32[]{:S(2)}, u32[]{:S(2)}) collective-permute-start(f32[3,4,4,1,128]{4,3,2,1,0:T(1,128)S(1)} %get-tuple-element.7), channel_id=1, source_target_pairs={{0,3},{1,0},{2,1},{3,2},{4,7},{5,4},{6,5},{7,6},{8,11},{9,8},{10,9... | collective-permute-start | bytes 73736 | tf_op jit(solution)/shard_map/ppermute | solution.py:50
where the time goes:
time: 69.3 us; the launch traced here: 69.1 us
  Pallas kernels  50.6 us (73%)
  starting transfers between devices  9.92 us (14%)
  waiting for transfers between devices  4.87 us (7%)
  other arithmetic  2.3 us (3%)
  local copies, waits for them, and re-layouts  0.78 us (1%)
    pallas_call x1, Pallas kernels, body(): step(ext.reshape(comps, -1, slots), positions.reshape(comps, own_cells, s...  50.6 us
    ppermute x2, starting transfers between devices, neighbour_layers(): lax.ppermute(last, name, [(d, (d + 1) % count) for d in range(count)])  5.73 us
    ppermute x2, waiting for transfers between devices, neighbour_layers(): lax.ppermute(first, name, [(d, (d - 1) % count) for d in range(count)])  2.31 us
    ppermute x1, starting transfers between devices, neighbour_layers(): lax.ppermute(jnp.concatenate([last, first], axis=axis), name, [(0, 1), (1...  2.09 us
    ppermute x2, starting transfers between devices, neighbour_layers(): lax.ppermute(first, name, [(d, (d - 1) % count) for d in range(count)])  2.09 us
  transfers between devices with their start and end apart: 5, of which 4 were waited for; matrix products, arithmetic and copies ran while one was open for 1% of the time, Pallas kernels for 0%

commit v1 on v0

v1 whole, which is shorter than its diff:
```python
import math
import jax
import jax.numpy as jnp
import numpy as np
from jax import lax
from jax.experimental import pallas as pl
from jax.experimental.pallas import tpu as pltpu
from jax.sharding import PartitionSpec as P

CELL_EDGE = 11.0
HALF_EDGE = 5.5
CUT_SQ = 25.0
WIDTH_DENSITY = 4.0
WIDTH_PAIR = 2.0
SCALE_DENSITY = 0.4
SCALE_PAIR = 0.3
DENSITY_REF = 1.0
TIME_STEP = 0.5
FAR = 4096.0
AXES = ("gx", "gy", "gz")

TOP_E = CUT_SQ / WIDTH_DENSITY
TOP = TOP_E / math.log(2.0)
SPREAD = math.sqrt(TOP / CUT_SQ)
DENSITY_SCALE = SCALE_DENSITY * math.exp(-TOP_E) / TOP**2
PAIR_SHIFT = 4.0 * TOP / CUT_SQ
DENSITY_SHIFT = 8.0 * TOP / CUT_SQ
FORCE_SCALE = -SCALE_PAIR * math.exp(-2.0 * TOP_E) / TOP**2
GRAD_SCALE = SCALE_DENSITY / (2.0 * SCALE_PAIR) * math.exp(TOP_E)

ROWS = 144
SPARE_ROWS = 32
LEFT_PARTS = (0, 0, 1, 0, 2, 1)
RIGHT_PARTS = (0, 1, 0, 2, 0, 1)
BLOCK = 8
TERMS = 6 * BLOCK
KEPT = 4 * BLOCK
NORM_AT = 3
ONE_AT = 4


def neighbour_layers(field, axis, name):
    count = lax.axis_size(name)
    size = field.shape[axis]
    first = lax.slice_in_dim(field, 0, 1, axis=axis)
    last = lax.slice_in_dim(field, size - 1, size, axis=axis)
    if count == 1:
        return last, first
    if count == 2:
        swapped = lax.ppermute(jnp.concatenate([last, first], axis=axis), name, [(0, 1), (1, 0)])
        return lax.slice_in_dim(swapped, 0, 1, axis=axis), lax.slice_in_dim(swapped, 1, 2, axis=axis)
    below = lax.ppermute(last, name, [(d, (d + 1) % count) for d in range(count)])
    above = lax.ppermute(first, name, [(d, (d - 1) % count) for d in range(count)])
    return below, above


def with_halo(field):
    for axis, name in enumerate(AXES):
        below, above = neighbour_layers(field, axis, name)
        field = jnp.concatenate([below, field, above], axis=axis)
    return field


def split_three(value):
    high = value.astype(jnp.bfloat16).astype(jnp.float32)
    rest = value - high
    middle = rest.astype(jnp.bfloat16).astype(jnp.float32)
    return high, middle, rest - middle


def rows_of(contract_a, contract_b, a, b):
    return lax.dot_general(
        a, b, (((contract_a,), (contract_b,)), ((), ())), preferred_element_type=jnp.float32
    )


def left_matrix():
    pick = np.zeros((KEPT, TERMS), np.float32)
    block_of = {0: 0, 1: 1, 2: 3}
    for block, part in enumerate(LEFT_PARTS):
        for comp in range(3):
            pick[block_of[part] * BLOCK + comp, block * BLOCK + comp] = 0.5
    for part, block in ((0, 0), (1, 1), (2, 3)):
        pick[ONE_AT, block * BLOCK + NORM_AT] = 1.0
    for part, block in ((0, 0), (1, 2), (2, 4)):
        pick[block_of[part] * BLOCK + NORM_AT, block * BLOCK + ONE_AT] = 1.0
    return pick


def block_step(extent, slots):
    inner_x, inner_y, inner_z = extent
    ext_y, ext_z = inner_y + 2, inner_z + 2
    cells = (inner_x + 2) * ext_y * ext_z
    vert_x, vert_y, vert_z = inner_x + 1, inner_y + 1, inner_z + 1
    verts = vert_x * vert_y * vert_z
    rows8 = verts * 8
    spare = cells * slots // SPARE_ROWS
    lanes = 8 * slots
    group_size = next(size for size in (3, 2, 1) if verts % size == 0)

    def cell_of(cx, cy, cz):
        return (cx * ext_y + cy) * ext_z + cz

    def vert_of(vx, vy, vz):
        return (vx * vert_y + vy) * vert_z + vz

    def corner_cells(v):
        vz = v % vert_z
        vy = (v // vert_z) % vert_y
        vx = v // (vert_z * vert_y)
        return [cell_of(vx + (k >> 2), vy + ((k >> 1) & 1), vz + (k & 1)) for k in range(8)]

    def kernel(ext_ref, pos_ref, vel_ref, live_ref, pick_ref, vel_out, moved_out,
               corner, cell_rows, dest, count_rows, right, left, left_now, listed_now, left_t, grad_row, dens_lane, grad_lane, totals,
               spare_left, spare_left_t, spare_grad, spare_vert, spare_count, count_scalars, count_sem):
        sub = lax.broadcasted_iota(jnp.int32, (8, slots), 0)
        fill = jnp.where(sub == ONE_AT, 1.0, 0.0)
        for c in range(cells):
            cell_rows[c * 8 : c * 8 + 8, :] = fill
            cell_rows[c * 8 : c * 8 + 3, :] = ext_ref[c]
        for v in range(verts):
            for kxy, c in enumerate(corner_cells(v)[::2]):
                for comp in range(3):
                    corner[comp, v * 8 + 2 * kxy : v * 8 + 2 * kxy + 2, :] = ext_ref[c : c + 2, comp, :]

        row_id = lax.broadcasted_iota(jnp.int32, (rows8, slots), 0)
        near = None
        for comp in range(3):
            upper = ((row_id >> (2 - comp)) & 1) == 1
            x = corner[comp]
            low = x < HALF_EDGE
            test = jnp.where(upper, jnp.where(low, 1.0, 0.0), jnp.where(low | (x > 0.5 * FAR), 0.0, 1.0))
            near = test if near is None else near * test
        near_b = near.astype(jnp.bfloat16)
        lane_a = lax.broadcasted_iota(jnp.int32, (slots, slots), 0)
        lane_b = lax.broadcasted_iota(jnp.int32, (slots, slots), 1)
        before = jnp.where(lane_a < lane_b, 1.0, 0.0).astype(jnp.bfloat16)
        prefix = jnp.dot(near_b, before, preferred_element_type=jnp.float32)
        total = jnp.dot(near_b, jnp.ones((slots, slots), jnp.bfloat16), preferred_element_type=jnp.float32)
        wide_a = lax.broadcasted_iota(jnp.int32, (rows8, rows8), 0)
        wide_b = lax.broadcasted_iota(jnp.int32, (rows8, rows8), 1)
        earlier = jnp.where((wide_a >> 3 == wide_b >> 3) & (wide_b < wide_a), 1.0, 0.0).astype(jnp.bfloat16)
        offset = jnp.dot(earlier, total.astype(jnp.bfloat16), preferred_element_type=jnp.float32)
        dest[...] = jnp.where(near > 0.5, prefix + offset, -1.0)
        most = jnp.max(offset + total)
        count_rows[...] = (offset + total).astype(jnp.int32)
        dens_lane[...] = jnp.zeros(dens_lane.shape, jnp.float32)

        scale = jnp.where(sub < 3, 2.0 * SPREAD, jnp.where(sub == ONE_AT, 1.0, 0.0))
        shifts = []
        for k in range(8):
            low_side = jnp.zeros((8, slots), jnp.float32)
            for comp in range(3):
                if not (k >> (2 - comp)) & 1:
                    low_side = jnp.where(sub == comp, 2.0 * SPREAD * CELL_EDGE, low_side)
            shifts.append(low_side)

        def terms_of(v):
            packed = []
            for k, c in enumerate(corner_cells(v)):
                x = cell_rows[pl.ds(pl.multiple_of(c * 8, 8), 8), :] * scale - shifts[k]
                square = jnp.sum(x * x, axis=0, keepdims=True)
                x = jnp.where(sub == NORM_AT, 0.5 * TOP + 0.25 - 0.25 * square, x)
                parts = split_three(x)
                packed.append([
                    jnp.concatenate([parts[RIGHT_PARTS[b]], parts[RIGHT_PARTS[b + 1]]], axis=0).astype(jnp.bfloat16)
                    for b in (0, 2, 4)
                ])
            return packed

        def store_terms(v, packed):
            for k in range(8):
                for pair in range(3):
                    right[v, 16 * pair : 16 * pair + 16, k * slots : (k + 1) * slots] = packed[k][pair]

        def list_of(v, first_row, rows):
            place = (dest[pl.ds(pl.multiple_of(v * 8, 8), 8), :] - first_row).astype(jnp.bfloat16)
            row = lax.broadcasted_iota(jnp.int32, (rows, slots), 0).astype(jnp.float32).astype(jnp.bfloat16)
            one, none = jnp.ones((), jnp.bfloat16), jnp.zeros((), jnp.bfloat16)
            chosen = jnp.concatenate([jnp.where(row == place[k : k + 1, :], one, none) for k in range(8)], axis=1)
            near_right = right[v, 0:KEPT, :]
            listed = rows_of(1, 1, chosen, near_right)
            return listed.astype(jnp.bfloat16), listed.T.astype(jnp.bfloat16)

        def lefts_of(listed):
            return jnp.dot(listed, pick_ref[...], preferred_element_type=jnp.float32).astype(jnp.bfloat16)

        def grad_of(density_sum):
            density = density_sum * DENSITY_SCALE
            return (2.0 * GRAD_SCALE) * (density - (SCALE_DENSITY + DENSITY_REF))

        def density_of(v, lefts, rows):
            near_cells = corner_cells(v)
            sums = None
            for pair in range(4):
                both = jnp.dot(
                    lefts, right[v, :, 2 * pair * slots : (2 * pair + 2) * slots], preferred_element_type=jnp.float32
                )
                for side in range(2):
                    s = jnp.maximum(both[:, side * slots : (side + 1) * slots], 0.0)
                    part = jnp.exp2(s) * (s * s)
                    sums = part if sums is None else sums + part
                    dens_lane[near_cells[2 * pair + side]] += jnp.sum(part.reshape(rows // 8, 8, slots), axis=0)
            grad = grad_of(jnp.sum(sums, axis=1, keepdims=True))
            return jnp.broadcast_to(grad, (rows, slots))

        last = verts // group_size - 1

        def group_of(g):
            return [jnp.minimum(g, last) * group_size + i for i in range(group_size)]

        def store_group(terms=None, lists=None, lefts=None):
            if lefts is not None:
                for i, v in enumerate(lefts[0]):
                    left[v] = lefts[1][i]
                    left_now[i] = lefts[1][i]
            if lists is not None:
                for i, v in enumerate(lists[0]):
                    listed_now[i] = lists[1][i][0]
                    left_t[v] = lists[1][i][1]
            if terms is not None:
                for i, v in enumerate(terms[0]):
                    store_terms(v, terms[1][i])

        def make(g, maker):
            return group_of(g), [maker(v) for v in group_of(g)]

        def make_lists(v):
            return list_of(v, 0.0, ROWS)

        def make_lefts(g):
            return group_of(g), [lefts_of(listed_now[i]) for i in range(group_size)]

        def visit(g, carry):
            now = [left_now[i] for i in range(group_size)]
            lefts = make_lefts(g + 1)
            grads = []
            lists = (group_of(g + 2), [])
            terms = (group_of(g + 3), [])
            for i in range(group_size):
                grads.append(density_of(g * group_size + i, now[i], ROWS))
                lists[1].append(make_lists(lists[0][i]))
                terms[1].append(terms_of(terms[0][i]))
            for i in range(group_size):
                grad_row[g * group_size + i] = grads[i]
            store_group(terms, lists, lefts)
            return carry

        for g in range(3):
            store_group(terms=make(g, terms_of))
        store_group(lists=make(0, make_lists))
        store_group(lefts=make_lefts(0))
        store_group(lists=make(1, make_lists))
        lax.fori_loop(0, verts // group_size, visit, 0)
        spare_count[0] = 0

        @pl.when(most > ROWS)
        def _():
            copy = pltpu.make_async_copy(count_rows, count_scalars, count_sem)
            copy.start()
            copy.wait()

            def visit_vert(v, carry):
                count = count_scalars[v * 8 + 7, 0]

                def chunk(t, inner):
                    slot = spare_count[0]
                    spare_count[0] = slot + 1
                    spare_vert[slot] = v
                    first = ROWS + t * SPARE_ROWS
                    listed, listed_t = list_of(v, first.astype(jnp.float32), SPARE_ROWS)
                    lefts = lefts_of(listed)
                    spare_left[slot] = lefts
                    spare_left_t[slot] = listed_t
                    spare_grad[slot] = density_of(v, lefts, SPARE_ROWS)
                    return inner

                more = jnp.maximum(count - ROWS + SPARE_ROWS - 1, 0) // SPARE_ROWS
                return lax.fori_loop(0, more, chunk, carry)

            lax.fori_loop(0, verts, visit_vert, 0)

        for c in range(cells):
            grad_lane[c] = jnp.broadcast_to(grad_of(jnp.sum(dens_lane[c], axis=0, keepdims=True)), (8, slots))

        def force_sums(v, k, c, lefts, listed_t, grads):
            s = jnp.dot(lefts, right[v, :, k * slots : (k + 1) * slots], preferred_element_type=jnp.float32)
            s = jnp.maximum(s, 0.0)
            fall = jnp.exp2(s)
            both = grads + grad_lane[c, 0:1, :]
            push = (fall * s) * (fall * (s + PAIR_SHIFT) + both * (s + DENSITY_SHIFT))
            high = push.astype(jnp.bfloat16)
            low = (push - high.astype(jnp.float32)).astype(jnp.bfloat16)
            return rows_of(1, 0, listed_t, high) + rows_of(1, 0, listed_t, low)

        def shares(sums, k):
            weight = sums[ONE_AT : ONE_AT + 1, :]
            out = []
            for comp in range(3):
                moment = sums[comp : comp + 1, :] + sums[BLOCK + comp : BLOCK + comp + 1, :]
                moment = (moment + sums[3 * BLOCK + comp : 3 * BLOCK + comp + 1, :]) * (0.5 / SPREAD)
                if not (k >> (2 - comp)) & 1:
                    moment = moment + CELL_EDGE * weight
                out.append(moment)
            return out + [weight]

        def visit_cell(n, carry):
            iz = n % inner_z
            iy = (n // inner_z) % inner_y
            ix = n // (inner_z * inner_y)
            c = cell_of(ix + 1, iy + 1, iz + 1)
            gathered = None
            for k in range(8):
                v = vert_of(ix + 1 - (k >> 2), iy + 1 - ((k >> 1) & 1), iz + 1 - (k & 1))
                part = shares(force_sums(v, k, c, left[v], left_t[v], grad_row[v]), k)
                gathered = part if gathered is None else [a + b for a, b in zip(gathered, part)]
            totals[c] = jnp.concatenate(gathered + [jnp.zeros((4, slots), jnp.float32)], axis=0)
            return carry

        lax.fori_loop(0, inner_x * inner_y * inner_z, visit_cell, 0, unroll=2)

        def spare_force(e, carry):
            v = spare_vert[e]
            for k, c in enumerate(corner_cells(v)):
                part = shares(force_sums(v, k, c, spare_left[e], spare_left_t[e], spare_grad[e]), k)
                totals[c] += jnp.concatenate(part + [jnp.zeros((4, slots), jnp.float32)], axis=0)
            return carry

        lax.fori_loop(0, spare_count[0], spare_force, 0)

        for ix in range(inner_x):
            for iy in range(inner_y):
                c = cell_of(ix + 1, iy + 1, 1)
                n = (ix * inner_y + iy) * inner_z
                for iz in range(inner_z):
                    alive = live_ref[n + iz : n + iz + 1, :]
                    both = totals[c + iz]
                    for comp in range(3):
                        x = pos_ref[comp, n + iz : n + iz + 1, :]
                        force = FORCE_SCALE * (both[comp : comp + 1, :] - x * both[3:4, :])
                        velocity = vel_ref[comp, n + iz : n + iz + 1, :] + TIME_STEP * force
                        velocity = jnp.where(alive > 0.5, velocity, 0.0)
                        vel_out[comp, n + iz : n + iz + 1, :] = velocity
                        moved_out[comp, n + iz : n + iz + 1, :] = TIME_STEP * velocity

    own_cells = inner_x * inner_y * inner_z
    vmem = pl.BlockSpec(memory_space=pltpu.VMEM)
    pairs = verts * 8 * ROWS * slots
    return pl.pallas_call(
        kernel,
        out_shape=(jax.ShapeDtypeStruct((3, own_cells, slots), jnp.float32),) * 2,
        in_specs=[vmem] * 5,
        out_specs=(vmem, vmem),
        scratch_shapes=[
            pltpu.VMEM((3, rows8, slots), jnp.float32),
            pltpu.VMEM((cells * 8, slots), jnp.float32),
            pltpu.VMEM((rows8, slots), jnp.float32),
            pltpu.VMEM((rows8, slots), jnp.int32),
            pltpu.VMEM((verts, TERMS, lanes), jnp.bfloat16),
            pltpu.VMEM((verts, ROWS, TERMS), jnp.bfloat16),
            pltpu.VMEM((group_size, ROWS, TERMS), jnp.bfloat16),
            pltpu.VMEM((group_size, ROWS, KEPT), jnp.bfloat16),
            pltpu.VMEM((verts, KEPT, ROWS), jnp.bfloat16),
            pltpu.VMEM((verts, ROWS, slots), jnp.float32),
            pltpu.VMEM((cells, 8, slots), jnp.float32),
            pltpu.VMEM((cells, 8, slots), jnp.float32),
            pltpu.VMEM((cells, 8, slots), jnp.float32),
            pltpu.VMEM((spare, SPARE_ROWS, TERMS), jnp.bfloat16),
            pltpu.VMEM((spare, KEPT, SPARE_ROWS), jnp.bfloat16),
            pltpu.VMEM((spare, SPARE_ROWS, slots), jnp.float32),
            pltpu.SMEM((spare,), jnp.int32),
            pltpu.SMEM((1,), jnp.int32),
            pltpu.SMEM((rows8, slots), jnp.int32),
            pltpu.SemaphoreType.DMA,
        ],
        compiler_params=pltpu.CompilerParams(vmem_limit_bytes=60 * 2**20),
        cost_estimate=pl.CostEstimate(flops=40 * pairs, bytes_accessed=4 * 3 * cells * slots, transcendentals=2 * pairs),
        name="block_step",
    )


def body(positions, velocities, counts):
    comps, size_x, size_y, size_z, slots = positions.shape
    own_cells = size_x * size_y * size_z
    slot_index = lax.broadcasted_iota(jnp.int32, counts.shape + (slots,), 3)
    live = slot_index < counts[..., None]
    shown = jnp.where(live[..., None, :], positions.transpose(1, 2, 3, 0, 4), FAR)
    ext = with_halo(shown)
    step = block_step((size_x, size_y, size_z), slots)
    velocity, moved = step(
        ext.reshape(-1, comps, slots),
        positions.reshape(comps, own_cells, slots),
        velocities.reshape(comps, own_cells, slots),
        live.astype(jnp.float32).reshape(own_cells, slots),
        jnp.asarray(left_matrix(), jnp.bfloat16),
    )
    return velocity.reshape(positions.shape), moved.reshape(positions.shape)


def solution(mesh):
    spec = P(None, *AXES, None)
    return jax.shard_map(
        body,
        mesh=mesh,
        in_specs=(spec, spec, P(*AXES)),
        out_specs=(spec, spec),
        check_vma=False,
    )
```

time: 69.3 us -> 47.1 us (0.68)
  the two profiles are of different devices: /device:TPU:1 before, /device:TPU:27 now
where the time goes in v1:
time: 47.1 us
  Pallas kernels  29.1 us (62%)
  waiting for transfers between devices  8.06 us (17%)
  starting transfers between devices  6.08 us (13%)
  other arithmetic  2.3 us (5%)
  local copies, waits for them, and re-layouts  0.89 us (2%)
  between operations  0.68 us (1%)
    pallas_call x1, Pallas kernels, body(): step(ext.reshape(-1, comps, slots), positions.reshape(comps, own_cells, s...  29.1 us
    ppermute x2, starting transfers between devices, neighbour_layers(): lax.ppermute(last, name, [(d, (d + 1) % count) for d in range(count)])  4.3 us
    ppermute x2, waiting for transfers between devices, neighbour_layers(): lax.ppermute(first, name, [(d, (d - 1) % count) for d in range(count)])  4.23 us
    ppermute x1, waiting for transfers between devices, neighbour_layers(): lax.ppermute(jnp.concatenate([last, first], axis=axis), name, [(0, 1), (1...  2.42 us
    ppermute x2, starting transfers between devices, neighbour_layers(): lax.ppermute(first, name, [(d, (d - 1) % count) for d in range(count)])  1.46 us
    ppermute x2, waiting for transfers between devices, neighbour_layers(): lax.ppermute(last, name, [(d, (d + 1) % count) for d in range(count)])  1.4 us
  transfers between devices with their start and end apart: 5, of which 5 were waited for; matrix products, arithmetic and copies ran while one was open for 2% of the time, Pallas kernels for 0%

profile of v1, /device:TPU:27, one launch (start us, length us, event | category | flops | bytes accessed | tf_op | source)
XLA Modules:
  0.0 47.1 jit_solution(10349431278007983696)
XLA Ops:
  0.6 0.8 %iota_compare_fusion.1 = pred[2,2,4,128]{3,2,1,0:T(4,128)(4,1)S(1)} fusion(s32[2,2,4]{2,1,0:T(2,128)} %param.6), kind=kLoop, calls=%fused_computation.10 | loop fusion | flops 2048 | bytes 2112 | tf_op jit(solution)/shard_map/lt | solution.py:386
  1.4 0.7 %select_bitcast_fusion = f32[2,2,4,3,128]{4,2,1,0,3:T(4,128)S(1)} fusion(f32[3,2,2,4,128]{4,3,2,1,0:T(4,128)} %param.4, pred[2,2,4,128]{3,2,1,0:T(4,128)(4,1)S(1)} %iota_compare_fusion.1), kind=kLoop, calls=%fused_computation.8 | loop fusion | flops 6144 | bytes 51200 | tf_op jit(solution)/shard_map/jit(_where)/select_n | solution.py:387
  2.2 0.3 collective-permute-start
  2.5 2.4 %collective-permute-done = f32[2,2,4,3,128]{4,2,1,0,3:T(4,128)S(1)} collective-permute-done((f32[2,2,4,3,128]{4,2,1,0,3:T(4,128)S(1)}, f32[2,2,4,3,128]{4,2,1,0,3:T(4,128)S(1)}, u32[]{:S(2)}, u32[]{:S(2)}) %collective-permute-start) | collective-permute-done | bytes 24608 | tf_op jit(solution)/shard_map/ppermute | solution.py:50
  4.9 0.0 copy-start
  5.0 0.1 collective-permute-start.1
  5.0 1.5 %collective-permute-start.2 = (f32[4,1,4,3,128]{4,2,1,0,3:T(4,128)S(1)}, f32[4,1,4,3,128]{4,2,1,0,3:T(4,128)S(1)}, u32[]{:S(2)}, u32[]{:S(2)}) collective-permute-start(f32[4,1,4,3,128]{4,2,1,0,3:T(4,128)S(1)} %get-tuple-element.9), channel_id=1, source_target_pairs={{0,12},{4,0},{8,4},{12,8},{1,13},{5,1},{9,5},{13,9},{2,14},{6,2},{... | collective-permute-start | bytes 73736 | tf_op jit(solution)/shard_map/ppermute | solution.py:53
  6.5 0.0 copy-done
  6.5 0.1 lt.21
  6.6 1.1 %collective-permute-done.1 = f32[4,1,4,3,128]{4,2,1,0,3:T(4,128)S(1)} collective-permute-done((f32[4,1,4,3,128]{4,2,1,0,3:T(4,128)S(1)}, f32[4,1,4,3,128]{4,2,1,0,3:T(4,128)S(1)}, u32[]{:S(2)}, u32[]{:S(2)}) %collective-permute-start.1) | collective-permute-done | bytes 24608 | tf_op jit(solution)/shard_map/ppermute | solution.py:52
  7.7 1.9 %collective-permute-done.2 = f32[4,1,4,3,128]{4,2,1,0,3:T(4,128)S(1)} collective-permute-done((f32[4,1,4,3,128]{4,2,1,0,3:T(4,128)S(1)}, f32[4,1,4,3,128]{4,2,1,0,3:T(4,128)S(1)}, u32[]{:S(2)}, u32[]{:S(2)}) %collective-permute-start.2) | collective-permute-done | bytes 24608 | tf_op jit(solution)/shard_map/ppermute | solution.py:53
  9.7 4.2 %collective-permute-start.3 = (f32[4,4,1,3,128]{4,2,1,0,3:T(1,128)S(1)}, f32[4,4,1,3,128]{4,2,1,0,3:T(1,128)S(1)}, u32[]{:S(2)}, u32[]{:S(2)}) collective-permute-start(f32[4,4,1,3,128]{4,2,1,0,3:T(1,128)S(1)} %get-tuple-element.6), channel_id=1, source_target_pairs={{0,1},{1,2},{2,3},{3,0},{4,5},{5,6},{6,7},{7,4},{8,9},{9,10},{10,1... | collective-permute-start | bytes 73736 | tf_op jit(solution)/shard_map/ppermute | solution.py:52
  13.9 0.0 collective-permute-start.4
  13.9 0.7 %fusion.live_ref = f32[16,128]{1,0:T(8,128)} fusion(s32[16]{0:T(128)S(1)} %lt.21), kind=kLoop, calls=%fused_computation.11 | loop fusion | flops 4096 | bytes 8256 | tf_op jit(solution)/shard_map/convert_element_type | solution.py:394
  14.6 0.3 collective-permute-done.3
  14.8 2.3 %collective-permute-done.4 = f32[4,4,1,3,128]{4,2,1,0,3:T(1,128)S(1)} collective-permute-done((f32[4,4,1,3,128]{4,2,1,0,3:T(1,128)S(1)}, f32[4,4,1,3,128]{4,2,1,0,3:T(1,128)S(1)}, u32[]{:S(2)}, u32[]{:S(2)}) %collective-permute-start.4) | collective-permute-done | bytes 24608 | tf_op jit(solution)/shard_map/ppermute | solution.py:53
  17.2 0.1 pad_maximum_fusion
  17.2 0.8 %copy.6 = f32[4,4,6,3,128]{4,3,2,1,0:T(4,128)} copy(f32[4,4,6,3,128]{4,2,1,0,3:T(8,128)S(1)} %pad_maximum_fusion) | data formatting | bytes 294912 | tf_op jit(solution)/shard_map/concatenate | solution.py:60
  18.0 29.1 %block_step.1 = (f32[3,16,128]{2,1,0:T(8,128)}, f32[3,16,128]{2,1,0:T(8,128)}) custom-call(f32[96,3,128]{2,1,0:T(4,128)} %bitcast.7, f32[3,16,128]{2,1,0:T(8,128)} %bitcast.8, f32[3,16,128]{2,1,0:T(8,128)} %bitcast.9, f32[16,128]{1,0:T(8,128)} %fusion.live_ref, bf16[32,48]{1,0:T(8,128)(2,1)} %constant.4.clone.pick_ref), custom_call_target="tpu_custom_call" | custom-call | flops 265420800 | bytes 147456 | tf_op jit(solution)/shard_map/block_step/pallas_call | solution.py:390
  (6 shorter events, 0.1 us)
Async XLA Ops:
  2.2 2.7 %collective-permute-start = (f32[2,2,4,3,128]{4,2,1,0,3:T(4,128)S(1)}, f32[2,2,4,3,128]{4,2,1,0,3:T(4,128)S(1)}, u32[]{:S(2)}, u32[]{:S(2)}) collective-permute-start(f32[2,2,4,3,128]{4,2,1,0,3:T(4,128)S(1)} %pad_maximum_fusion.7), channel_id=1, source_target_pairs={{0,16},{16,0},{1,17},{17,1},{2,18},{18,2},{3,19},{19,3},{4,20},{20... | collective-permute-start | bytes 73736 | tf_op jit(solution)/shard_map/ppermute | solution.py:50
  4.9 1.5 %copy-start = (s32[2,2,4]{2,1,0:T(2,128)S(1)}, s32[2,2,4]{2,1,0:T(2,128)}, u32[]{:S(2)}) copy-start(s32[2,2,4]{2,1,0:T(2,128)} %param.6) | copy-start | bytes 196
  5.0 2.7 %collective-permute-start.1 = (f32[4,1,4,3,128]{4,2,1,0,3:T(4,128)S(1)}, f32[4,1,4,3,128]{4,2,1,0,3:T(4,128)S(1)}, u32[]{:S(2)}, u32[]{:S(2)}) collective-permute-start(f32[4,1,4,3,128]{4,2,1,0,3:T(4,128)S(1)} %get-tuple-element.8), channel_id=1, source_target_pairs={{0,4},{4,8},{8,12},{12,0},{1,5},{5,9},{9,13},{13,1},{2,6},{6,10},{... | collective-permute-start | bytes 73736 | tf_op jit(solution)/shard_map/ppermute | solution.py:52
  5.0 4.6 %collective-permute-start.2 = (f32[4,1,4,3,128]{4,2,1,0,3:T(4,128)S(1)}, f32[4,1,4,3,128]{4,2,1,0,3:T(4,128)S(1)}, u32[]{:S(2)}, u32[]{:S(2)}) collective-permute-start(f32[4,1,4,3,128]{4,2,1,0,3:T(4,128)S(1)} %get-tuple-element.9), channel_id=1, source_target_pairs={{0,12},{4,0},{8,4},{12,8},{1,13},{5,1},{9,5},{13,9},{2,14},{6,2},{... | collective-permute-start | bytes 73736 | tf_op jit(solution)/shard_map/ppermute | solution.py:53
  9.7 5.2 %collective-permute-start.3 = (f32[4,4,1,3,128]{4,2,1,0,3:T(1,128)S(1)}, f32[4,4,1,3,128]{4,2,1,0,3:T(1,128)S(1)}, u32[]{:S(2)}, u32[]{:S(2)}) collective-permute-start(f32[4,4,1,3,128]{4,2,1,0,3:T(1,128)S(1)} %get-tuple-element.6), channel_id=1, source_target_pairs={{0,1},{1,2},{2,3},{3,0},{4,5},{5,6},{6,7},{7,4},{8,9},{9,10},{10,1... | collective-permute-start | bytes 73736 | tf_op jit(solution)/shard_map/ppermute | solution.py:52
  13.9 3.3 %collective-permute-start.4 = (f32[4,4,1,3,128]{4,2,1,0,3:T(1,128)S(1)}, f32[4,4,1,3,128]{4,2,1,0,3:T(1,128)S(1)}, u32[]{:S(2)}, u32[]{:S(2)}) collective-permute-start(f32[4,4,1,3,128]{4,2,1,0,3:T(1,128)S(1)} %get-tuple-element.7), channel_id=1, source_target_pairs={{0,3},{1,0},{2,1},{3,2},{4,7},{5,4},{6,5},{7,6},{8,11},{9,8},{10,9... | collective-permute-start | bytes 73736 | tf_op jit(solution)/shard_map/ppermute | solution.py:53
